TPU v7x, 32 devices: a whole 2x2x4 slice. The times are simulated.
32 devices in a mesh: dom: 8 (over y, x, core), col: 4 (over z).
Axes of the slice: x: 2, y: 2, z: 4, core: 2. Of those that a mesh axis runs over, the one named last changes fastest.
Arguments:
- basis_panel: bfloat16 [256, 163840], P('col', 'dom'), may hold values from -12 to 12
- jacobian: bfloat16 [2, 320, 16384], P(None, None, 'dom'), may hold values from -0.25 to 0.25
- neighbors: int32 [512, 2], P('dom'), may hold values from 0 to 63
- sample_rows: int32 [16384], P('dom'), may hold values from 0 to 8191, as said below
- residual_parts: float32 [16384], P('dom'), may hold values from -48 to 48
Outputs:
- jacobian_basis: float32 [256, 8192], P('col', 'dom')
- sampled_residual: float32 [8192], P('dom')
- reduced_step: float32 [256], P('col')
Inputs may be any that keep to these rules, and one draw needn't show every extreme that they name: `sample_rows`: for each index d of dom, its 2048 entries name each of its own rows d * 1024 to d * 1024 + 1023 exactly once; the other 1024 entries name rows owned by the 7 indices d + 1 to d + 7 of dom, cyclically, at most 256 to any one of them and exactly 256 to one of them. `neighbors`: each entry is an element of the same index of dom, counted from that index's first element.
All inputs are finite; a program needn't handle non-finite values.
Results may differ from a plain program's by a relative error of at most 0.0003.
Values sent between devices are 32-bit elements; how exact they have to be, the bound alone decides.
A program may use at most 64 MiB of HBM per device.

v0:
```python
import jax
import jax.numpy as jnp
from jax import lax
from jax.sharding import PartitionSpec as P

NODE = 320
NB = 2
RS = 32
ROWS_DEV = 1024
CAP = 256


def element_products(basis_panel, jacobian, neighbors):
    panel_width = basis_panel.shape[0]
    element_count = neighbors.shape[0]
    panels = basis_panel.reshape(panel_width, element_count, NODE)
    blocks = jacobian.reshape(NB, NODE, element_count, RS)
    summed = jnp.zeros((panel_width, element_count, RS), jnp.float32)
    for coupled in range(NB):
        picked = jnp.take(panels, neighbors[:, coupled], axis=1)
        summed = summed + jnp.einsum(
            "cep,per->cer", picked, blocks[coupled], preferred_element_type=jnp.float32
        )
    return summed.reshape(panel_width, element_count * RS)


def body(basis_panel, jacobian, neighbors, sample_rows, residual_parts):
    dom_count = lax.axis_size("dom")
    self_index = lax.axis_index("dom")
    partial_value = element_products(basis_panel, jacobian, neighbors)
    panel_width = partial_value.shape[0]
    owners = sample_rows // ROWS_DEV
    local_rows = sample_rows % ROWS_DEV
    is_local = owners == self_index
    own_rows = jnp.where(is_local, local_rows, ROWS_DEV)
    jacobian_basis = (
        jnp.zeros((panel_width, ROWS_DEV), jnp.float32)
        .at[:, own_rows]
        .add(partial_value, mode="drop")
    )
    sampled_residual = (
        jnp.zeros((ROWS_DEV,), jnp.float32).at[own_rows].add(residual_parts, mode="drop")
    )
    matches = (owners[None, :] == jnp.arange(dom_count, dtype=jnp.int32)[:, None]).astype(jnp.int32)
    ranking = jnp.sum(matches * (jnp.cumsum(matches, axis=1) - 1), axis=0)
    row_values = local_rows.astype(jnp.float32)
    target_slot = jnp.where(is_local, dom_count * CAP, owners * CAP + ranking)
    send_values = (
        jnp.zeros((panel_width, dom_count * CAP), jnp.float32)
        .at[:, target_slot]
        .set(partial_value, mode="drop")
        .reshape(panel_width, dom_count, CAP)
    )
    send_residual = (
        jnp.zeros((dom_count * CAP,), jnp.float32)
        .at[target_slot]
        .set(residual_parts, mode="drop")
        .reshape(1, dom_count, CAP)
    )
    send_rows = (
        jnp.full((dom_count * CAP,), float(ROWS_DEV), jnp.float32)
        .at[target_slot]
        .set(row_values, mode="drop")
        .reshape(1, dom_count, CAP)
    )
    arrived_values, arrived_residual, arrived_rows = (
        lax.all_to_all(send_values, "dom", split_axis=1, concat_axis=1, tiled=True),
        lax.all_to_all(send_residual, "dom", split_axis=1, concat_axis=1, tiled=True),
        lax.all_to_all(send_rows, "dom", split_axis=1, concat_axis=1, tiled=True),
    )
    landing = arrived_rows.reshape(-1).astype(jnp.int32)
    jacobian_basis = jacobian_basis.at[:, landing].add(
        arrived_values.reshape(panel_width, -1), mode="drop"
    )
    sampled_residual = sampled_residual.at[landing].add(arrived_residual.reshape(-1), mode="drop")
    gram_panel = jnp.einsum(
        "cr,kr->ck",
        jacobian_basis,
        lax.all_gather(jacobian_basis, "col", axis=0, tiled=True),
        precision=lax.Precision.HIGHEST,
        preferred_element_type=jnp.float32,
    )
    gradient_panel = jnp.einsum(
        "cr,r->c", jacobian_basis, sampled_residual, precision=lax.Precision.HIGHEST
    )
    gram_panel, gradient_panel = lax.psum((gram_panel, gradient_panel), "dom")
    gram_matrix, gradient = (
        lax.all_gather(gram_panel, "col", axis=0, tiled=True),
        lax.all_gather(gradient_panel, "col", axis=0, tiled=True),
    )
    factor = jnp.linalg.cholesky(gram_matrix)
    forward = lax.linalg.triangular_solve(factor, gradient[:, None], left_side=True, lower=True)
    backward = lax.linalg.triangular_solve(
        factor, forward, left_side=True, lower=True, transpose_a=True
    )
    full_step = -backward[:, 0]
    reduced_step = lax.dynamic_slice_in_dim(
        full_step, lax.axis_index("col") * panel_width, panel_width
    )
    return (jacobian_basis, sampled_residual, reduced_step)


def solution(mesh):
    placed = (P("col", "dom"), P(None, None, "dom"), P("dom", None), P("dom"), P("dom"))
    return jax.shard_map(
        body,
        mesh=mesh,
        in_specs=placed,
        out_specs=(P("col", "dom"), P("dom"), P("col")),
        check_vma=False,
    )
```

profile of v0, /device:TPU:0, one launch (start us, length us, event | category | flops | bytes accessed | tf_op | source)
XLA Modules:
  0.0 269.4 jit_solution(11350941554137800670)
XLA Ops:
  7.2 0.7 fusion.44
  7.9 2.3 reduce-window.6
  10.2 0.3 slice_reduce_fusion
  10.5 0.2 reduce-window.9
  10.6 0.1 select_reduce_fusion.2
  10.7 0.7 compare_select_fusion.1
  11.5 8.6 %scatter_custom_fusion.1 = f32[2048]{0:T(1024)} fusion(s32[2048]{0:T(1024)S(1)} %compare_select_fusion.1, f32[2048]{0:T(1024)S(1)} %get-tuple-element.47, f32[]{:T(128)} %constant.144.clone.1), kind=kCustom, calls=%fused_computation.75 | custom fusion | bytes 8196 | tf_op jit(solution)/shard_map/scatter | solution.py:63
  20.1 5.2 %all-to-all-start = ((f32[1,8,256]{2,0,1:T(1,128)}), f32[1,8,256]{2,0,1:T(1,128)S(1)}, u32[]{:S(2)}, u32[]{:S(2)}) async-start(f32[1,8,256]{2,0,1:T(1,128)} %bitcast.11), calls=%async_computation | async-start | bytes 16384 | tf_op jit(solution)/shard_map/all_to_all | solution.py:69
  25.3 3.0 %fusion.47 = (bf16[1,320,2048]{2,1,0:T(8,128)(2,1)}, bf16[1,320,2048]{2,1,0:T(8,128)(2,1)S(1)}) fusion(bf16[2,320,2048]{2,1,0:T(8,128)(2,1)} %param.8), kind=kLoop, calls=%fused_computation.101 | loop fusion | bytes 5242880 | tf_op jit(solution)/shard_map/slice | solution.py:22
  28.3 1.5 copy.36
  29.9 6.2 %reshape.129 = bf16[64,64,320]{2,1,0:T(8,128)(2,1)} reshape(bf16[64,20480]{1,0:T(8,128)(2,1)} %param.7) | data formatting | bytes 5242880 | tf_op jit(solution)/shard_map/reshape | solution.py:16
  36.1 3.8 %copy.33 = bf16[64,64,320]{2,0,1:T(8,128)(2,1)S(1)} copy(bf16[64,64,320]{2,1,0:T(8,128)(2,1)} %reshape.129) | data formatting | bytes 5242880 | tf_op jit(solution)/shard_map/reshape | solution.py:16
  39.9 2.6 copy.34
  42.5 2.6 gather_fusion.1
  45.2 2.7 gather_fusion
  47.8 3.8 %fusion = f32[64,64,32]{1,2,0:T(8,128)S(1)} fusion(bf16[320,64,32]{0,2,1:T(8,128)(2,1)} %bitcast.125, bf16[64,64,320]{2,1,0:T(8,128)(2,1)} %gather_fusion.1, pred[64]{0:T(512)(128)(4,1)S(1)} %get-tuple-element.50), kind=kOutput, calls=%fused_computation.11 | convolution fusion | flops 85196800 | bytes 4456512 | tf_op jit(solution)/shard_map/cep,per->cer/dot_general | solution.py:21
  51.6 1.3 fusion.10
  52.9 5.8 %scatter_custom_fusion.2 = f32[64,2048]{0,1:T(8,128)S(1)} fusion(s32[2048]{0:T(1024)S(1)} %compare_select_fusion.1, f32[2048,64]{1,0:T(8,128)S(1)} %bitcast.132, f32[]{:T(128)} %constant.135.clone.1), kind=kCustom, calls=%fused_computation.33 | custom fusion | bytes 524292 | tf_op jit(solution)/shard_map/scatter | solution.py:51
  58.8 1.1 copy.37
  59.9 4.2 %all-to-all-start.1 = ((f32[64,8,256]{2,0,1:T(8,128)}), f32[64,8,256]{2,0,1:T(8,128)S(1)}, u32[]{:S(2)}, u32[]{:S(2)}) async-start(f32[64,8,256]{2,0,1:T(8,128)} %copy.37), calls=%async_computation.1 | async-start | bytes 1048576 | tf_op jit(solution)/shard_map/all_to_all | solution.py:67
  64.1 0.2 all-gather.2.cloned.1.call-start
  64.3 11.6 %scatter_custom_fusion = f32[64,1024]{0,1:T(8,128)S(1)} fusion(s32[2048]{0:T(1024)S(1)} %get-tuple-element.49, f32[2048,64]{1,0:T(8,128)S(1)} %bitcast.133, f32[]{:T(128)} %constant.135.clone.1), kind=kCustom, calls=%fused_computation.39 | custom fusion | flops 131072 | bytes 262148 | tf_op jit(solution)/shard_map/scatter-add | solution.py:39
  76.0 0.3 copy.39
  76.4 0.0 copy-start.4
  76.4 11.7 %scatter_fusion = f32[64,1024]{0,1:T(8,128)S(1)} fusion(f32[64,1024]{0,1:T(8,128)S(1)} %scatter_custom_fusion, s32[2048]{0:T(1024)S(1)} %bitcast.127, f32[2048,64]{1,0:T(8,128)S(1)} %copy.39), kind=kCustom, calls=%fused_computation.5 | custom fusion | flops 131072 | bytes 1581056 | tf_op jit(solution)/shard_map/scatter-add | solution.py:72
  88.1 0.9 copy.42
  89.0 0.0 all-gather.2.cloned.1.call-update
  89.0 8.8 %scatter_custom_fusion.5 = f32[2048]{0:T(1024)} fusion(s32[2048]{0:T(1024)S(1)} %compare_select_fusion.1, f32[2048]{0:T(1024)} %param.11, f32[]{:T(128)} %constant.135.clone.1), kind=kCustom, calls=%fused_computation.73 | custom fusion | bytes 8704 | tf_op jit(solution)/shard_map/scatter | solution.py:57
  97.7 4.0 %all-to-all-start.2 = ((f32[1,8,256]{2,0,1:T(1,128)}), f32[1,8,256]{2,0,1:T(1,128)S(1)}, u32[]{:S(2)}, u32[]{:S(2)}) async-start(f32[1,8,256]{2,0,1:T(1,128)} %bitcast.18), calls=%async_computation.2 | async-start | bytes 16384 | tf_op jit(solution)/shard_map/all_to_all | solution.py:68
  101.7 0.0 all-reduce.4.cloned.1.call-start
  101.8 11.6 %scatter_custom_fusion.4 = f32[1024]{0:T(1024)S(1)} fusion(s32[2048]{0:T(1024)S(1)} %get-tuple-element.49, f32[2048]{0:T(1024)} %param.11, f32[]{:T(128)} %constant.135.clone.1), kind=kCustom, calls=%fused_computation.80 | custom fusion | flops 2048 | bytes 4608 | tf_op jit(solution)/shard_map/scatter-add | solution.py:42
  113.5 0.6 dynamic-slice.4
  114.7 13.0 %scatter_fusion.1 = f32[1024]{0:T(1024)S(1)} fusion(f32[1024]{0:T(1024)S(1)} %scatter_custom_fusion.4, s32[2048]{0:T(1024)S(1)} %bitcast.128, f32[2048]{0:T(1024)S(1)} %bitcast.129), kind=kCustom, calls=%fused_computation.8 | custom fusion | flops 2048 | bytes 32768 | tf_op jit(solution)/shard_map/scatter-add | solution.py:75
  127.8 0.0 all-gather.2.cloned.1.call-done
  127.8 2.9 %fusion.48 = f32[64,256]{1,0:T(8,128)} fusion(f32[64,1024]{0,1:T(8,128)S(1)} %scatter_fusion, f32[256,1024]{1,0:T(8,128)} %all-gather.2.cloned.1.call-done), kind=kOutput, calls=%fused_computation.102 | convolution fusion | flops 201326592 | bytes 1376256 | tf_op jit(solution)/shard_map/cr,kr->ck/dot_general | solution.py:76
  130.7 0.0 all-reduce.4.cloned.1.call-update
  130.7 0.4 convolution_bitcast_fusion.5
  131.1 14.4 %psum.15 = f32[64]{0:T(128)S(1)} all-reduce(f32[64]{0:T(128)S(1)} %convolution_bitcast_fusion.5), channel_id=1, replica_groups=mesh['dom'=8,'col'=4] {'dom'}, use_global_device_ids=true, to_apply=%region_15.17 | all-reduce | flops 64 | bytes 512 | tf_op jit(solution)/shard_map/psum | solution.py:86
  145.5 0.2 dynamic-update-slice.11
  145.7 11.9 %all-reduce.1 = f32[256]{0:T(256)S(1)} all-reduce(f32[256]{0:T(256)S(1)} %dynamic-update-slice.11), channel_id=1, replica_groups=mesh['dom'=8,'col'=4] {'col'}, use_global_device_ids=true, to_apply=%add.1 | all-reduce | flops 256 | bytes 2048
  157.6 28.1 %all-reduce.4.cloned.1.call-done = f32[64,256]{1,0:T(8,128)} async-done(((f32[64,256]{1,0:T(8,128)}), f32[64,256]{1,0:T(8,128)}) %all-reduce.4.cloned.1.call-update) | async-done | bytes 65552 | tf_op jit(solution)/shard_map/psum | solution.py:86
  185.7 14.3 %all_gather.10 = f32[256,256]{1,0:T(8,128)S(1)} all-gather(f32[64,256]{1,0:T(8,128)} %all-reduce.4.cloned.1.call-done), channel_id=1, replica_groups=mesh['dom'=8,'col'=4] {'col'}, dimensions={0}, use_global_device_ids=true | all-gather | bytes 327680 | tf_op jit(solution)/shard_map/all_gather | solution.py:88
  200.1 0.1 copy.41
  200.3 11.7 %cholesky.50 = f32[128,128]{1,0:T(8,128)S(1)} custom-call(f32[128,128]{1,0:T(8,128)S(1)} %cholesky.118), custom_call_target="Cholesky" | custom-call | tf_op jit(solution)/shard_map/jit(cholesky)/cholesky | solution.py:91
  212.0 9.8 %custom-call.16 = f32[1,128,128]{1,2,0:T(8,128)S(1)} custom-call(f32[1,128,128]{2,1,0:T(8,128)S(1)} %get-tuple-element.46), custom_call_target="InvertDiagBlocksLowerTriangular" | custom-call | tf_op jit(solution)/shard_map/jit(cholesky)/cholesky | solution.py:91
  221.8 0.2 constant_dynamic-update-slice_fusion
  222.1 0.3 convolution_subtract_fusion
  222.3 11.7 %cholesky.105 = f32[128,128]{1,0:T(8,128)S(1)} custom-call(f32[128,128]{1,0:T(8,128)S(1)} %convolution_subtract_fusion), custom_call_target="Cholesky" | custom-call | tf_op jit(solution)/shard_map/jit(cholesky)/cholesky | solution.py:91
  234.0 0.7 compare_reduce_fusion.1
  234.8 0.6 compare_reduce_fusion
  236.7 0.1 triangular_solve.70
  236.8 4.3 %while.1 = (s32[]{:T(128)}, f32[256,256]{1,0:T(8,128)S(1)}, s32[2,2]{1,0:T(2,128)S(1)}, f32[2,128,128]{2,1,0:T(8,128)S(1)}, s32[]{:T(128)}) while((s32[]{:T(128)}, f32[256,256]{1,0:T(8,128)S(1)}, s32[2,2]{1,0:T(2,128)S(1)}, f32[2,128,128]{2,1,0:T(8,128)S(1)}, s32[]{:T(128)}) %tuple.40), condition=%wide.while_cond, body=%wide.while_body.sunk | while | flops 2 | bytes 131189 | solution.py:93
  237.0 0.7 fusion.62
  237.7 1.3 bitcast_dynamic-update-slice_fusion.2
  239.1 0.7 fusion.62
  239.7 1.3 bitcast_dynamic-update-slice_fusion.2
  241.1 19.7 %custom-call.17 = f32[2,128,128]{1,2,0:T(8,128)S(1)} custom-call(f32[2,128,128]{2,1,0:T(8,128)S(1)} %get-tuple-element.11), custom_call_target="InvertDiagBlocksLowerTriangular" | custom-call | tf_op jit(solution)/shard_map/triangular_solve | solution.py:93
  260.8 0.2 fusion.26
  260.9 0.2 fusion.16
  261.1 0.2 convolution_bitcast_fusion.3
  261.3 0.2 convolution_bitcast_fusion.2
  261.5 0.2 fusion.14
  261.7 0.2 convolution_bitcast_fusion
  261.9 0.6 negate_bitcast_fusion
  (29 shorter events, 0.3 us)
Async XLA Ops:
  20.1 39.8 %all-to-all-start = ((f32[1,8,256]{2,0,1:T(1,128)}), f32[1,8,256]{2,0,1:T(1,128)S(1)}, u32[]{:S(2)}, u32[]{:S(2)}) async-start(f32[1,8,256]{2,0,1:T(1,128)} %bitcast.11), calls=%async_computation | async-start | bytes 16384 | tf_op jit(solution)/shard_map/all_to_all | solution.py:69
  36.1 3.8 %copy-start.3 = (s32[64,2]{0,1:T(2,128)S(1)}, s32[64,2]{0,1:T(2,128)}, u32[]{:S(2)}) copy-start(s32[64,2]{0,1:T(2,128)} %param.9) | copy-start | bytes 1540
  47.8 3.8 %copy-start.1 = (bf16[64,64,320]{2,1,0:T(8,128)(2,1)S(1)}, bf16[64,64,320]{2,1,0:T(8,128)(2,1)}, u32[]{:S(2)}) copy-start(bf16[64,64,320]{2,1,0:T(8,128)(2,1)} %gather_fusion) | copy-start | bytes 7864324
  47.8 3.8 %copy-start.2 = (bf16[1,320,2048]{1,2,0:T(8,128)(2,1)S(1)}, bf16[1,320,2048]{1,2,0:T(8,128)(2,1)}, u32[]{:S(2)}) copy-start(bf16[1,320,2048]{1,2,0:T(8,128)(2,1)} %copy.34) | copy-start | bytes 3932164
  59.9 16.1 %all-to-all-start.1 = ((f32[64,8,256]{2,0,1:T(8,128)}), f32[64,8,256]{2,0,1:T(8,128)S(1)}, u32[]{:S(2)}, u32[]{:S(2)}) async-start(f32[64,8,256]{2,0,1:T(8,128)} %copy.37), calls=%async_computation.1 | async-start | bytes 1048576 | tf_op jit(solution)/shard_map/all_to_all | solution.py:67
  64.1 63.7 %all-gather.2.cloned.1.call-start = ((), (), s32[]{:S(2)}) async-start(), calls=%async_computation.3 | async-start | bytes 1310720 | tf_op jit(solution)/shard_map/all_gather | solution.py:79
  76.4 37.1 %copy-start.4 = (u32[32]{0:T(128)S(1)}, u32[32]{0:T(128)}, u32[]{:S(2)}) copy-start(u32[32]{0:T(128)} %constant.171) | copy-start | bytes 388
  97.7 16.9 %all-to-all-start.2 = ((f32[1,8,256]{2,0,1:T(1,128)}), f32[1,8,256]{2,0,1:T(1,128)S(1)}, u32[]{:S(2)}, u32[]{:S(2)}) async-start(f32[1,8,256]{2,0,1:T(1,128)} %bitcast.18), calls=%async_computation.2 | async-start | bytes 16384 | tf_op jit(solution)/shard_map/all_to_all | solution.py:68
  101.7 84.0 %all-reduce.4.cloned.1.call-start = ((), (), s32[]{:S(2)}) async-start(), calls=%async_computation.4 | async-start | bytes 131072 | tf_op jit(solution)/shard_map/psum | solution.py:86
  127.7 109.0 %copy-start = (f32[1024]{0:T(1024)}, f32[1024]{0:T(1024)S(1)}, u32[]{:S(2)}) copy-start(f32[1024]{0:T(1024)S(1)} %scatter_fusion.1) | copy-start | bytes 12292
Sparse Core Ops, SparseCore 0:
  89.1 29.4 all-gather.1
  130.8 54.8 all-reduce.3
where the time goes:
time: 270 us; the launch traced here: 269 us
  other arithmetic  107 us (40%)
  local copies, waits for them, and re-layouts  53.5 us (20%)
  blocking collectives  40.7 us (15%)
  waiting for transfers between devices  28.1 us (10%)
  between operations  16.2 us (6%)
  starting transfers between devices  13.6 us (5%)
  matrix products  9.92 us (4%)
    another operation x7, other arithmetic, body(): factor = jnp.linalg.cholesky(gram_matrix)  34.7 us
    psum x1, waiting for transfers between devices, body(): gram_panel, gradient_panel = lax.psum((gram_panel, gradient_panel), 'dom')  28.1 us
    another operation x3, other arithmetic, body(): lax.linalg.triangular_solve(factor, forward, left_side=True, lower=True,...  19.7 us
    psum x1, blocking collectives, body(): gram_panel, gradient_panel = lax.psum((gram_panel, gradient_panel), 'dom')  14.4 us
    all_gather x1, blocking collectives, body(): lax.all_gather(gram_panel, 'col', axis=0, tiled=True)  14.3 us
    scatter-add x1, other arithmetic, body(): sampled_residual.at[landing].add(arrived_residual.reshape(-1), mode='drop')  13 us
    unnamed x1, blocking collectives  11.9 us
    scatter-add x1, other arithmetic, body(): jacobian_basis.at[:, landing]  11.7 us
  transfers between devices with their start and end apart: 5, of which 1 were waited for; matrix products, arithmetic and copies ran while one was open for 30% of the time, Pallas kernels for 0%

commit v1 on v0

v1 whole, which is shorter than its diff:
```python
import functools

import jax
import jax.numpy as jnp
from jax import lax
from jax.experimental import pallas as pl
from jax.experimental.pallas import tpu as pltpu
from jax.sharding import PartitionSpec as P

ROWS_DEV = 1024
CAP = 256
LANES = 128
HIGHEST = lax.Precision.HIGHEST
F32 = jnp.float32
BF16 = jnp.bfloat16


def iota(shape, dim):
    return lax.broadcasted_iota(jnp.int32, shape, dim)


def dot_nn(a, b, precision=None):
    return lax.dot_general(
        a, b, (((1,), (0,)), ((), ())), precision=precision, preferred_element_type=F32
    )


def dot_nt(a, b, precision=None):
    return lax.dot_general(
        a, b, (((1,), (1,)), ((), ())), precision=precision, preferred_element_type=F32
    )


def dot_tn(a, b, precision=None):
    return lax.dot_general(
        a, b, (((0,), (0,)), ((), ())), precision=precision, preferred_element_type=F32
    )


def split_values(x):
    high = x.astype(BF16)
    return high, (x - high.astype(F32)).astype(BF16)


def split_extra(x):
    high = x.astype(BF16).astype(F32)
    middle = (x - high).astype(BF16).astype(F32)
    low = x - high - middle
    return jnp.concatenate([high, middle, low, jnp.zeros_like(x)], axis=0).astype(BF16)


def join(found, width):
    values = found[:width] + found[width : 2 * width]
    base = 2 * width
    extra = found[base : base + 8] + found[base + 8 : base + 16] + found[base + 16 : base + 24]
    return jnp.concatenate([values, extra], axis=0)


def pick(terms, targets, base):
    spots = iota((CAP, targets.shape[1]), 0) + base
    return dot_nt(terms, (spots == targets).astype(F32).astype(BF16))


def product_kernel(
    dom_count, self_ref, links_ref, panel_ref, blocks_ref, rows_ref, parts_ref,
    local_ref, send_ref, panels, terms,
):
    width = panel_ref.shape[0]
    coupled_count, node, entries = blocks_ref.shape
    elements = links_ref.shape[0]
    rs = entries // elements
    group = LANES // rs

    @pl.loop(0, elements // 2)
    def _(pair):
        window = panel_ref[:, pl.ds(pl.multiple_of(pair * 2 * node, LANES), 2 * node)]
        panels[2 * pair] = window[:, :node]
        panels[2 * pair + 1] = window[:, node:]

    lane_element = iota((width, LANES), 1) // rs

    @pl.loop(0, elements // group)
    def _(block):
        columns = pl.ds(pl.multiple_of(block * LANES, LANES), LANES)
        total = jnp.zeros((group * width, LANES), F32)
        for coupled in range(coupled_count):
            picked = jnp.concatenate(
                [panels[links_ref[block * group + q, coupled]] for q in range(group)], axis=0
            )
            total = total + dot_nn(picked, blocks_ref[coupled, :, columns])
        out = total[:width]
        for q in range(1, group):
            out = jnp.where(lane_element == q, total[q * width : (q + 1) * width], out)
        high, low = split_values(out)
        terms[:width, columns] = high
        terms[width : 2 * width, columns] = low

    own = self_ref[0]
    shift = ROWS_DEV.bit_length() - 1
    match_rows = max(16, dom_count)
    before = (iota((LANES, LANES), 0) < iota((LANES, LANES), 1)).astype(F32).astype(BF16)
    carry = jnp.zeros((match_rows, 1), F32)
    targets = []
    for start in range(0, entries, LANES):
        rows = rows_ref[:, start : start + LANES]
        owner = rows >> shift
        local_row = rows & (ROWS_DEV - 1)
        matches = (iota((match_rows, LANES), 0) == owner).astype(F32)
        ranks = jnp.sum(
            matches * (dot_nn(matches.astype(BF16), before) + carry), axis=0, keepdims=True
        ).astype(jnp.int32)
        carry = carry + jnp.sum(matches, axis=1, keepdims=True)
        targets.append(jnp.where(owner == own, local_row, ROWS_DEV + owner * CAP + ranks))
    targets = jnp.concatenate(targets, axis=1)

    row_values = (rows_ref[...] & (ROWS_DEV - 1)).astype(F32)
    which = iota((8, entries), 0)
    extra = jnp.where(which == 0, parts_ref[...], jnp.where(which == 1, row_values, 0.0))
    terms[2 * width :, :] = split_extra(extra)

    @pl.loop(0, ROWS_DEV // CAP)
    def _(tile):
        base = tile * CAP
        local_ref[:, pl.ds(pl.multiple_of(base, CAP), CAP)] = join(
            pick(terms[...], targets, base), width
        )

    @pl.loop(0, dom_count)
    def _(owner):
        send_ref[owner] = join(pick(terms[...], targets, ROWS_DEV + owner * CAP), width)


def assemble_kernel(local_ref, arrived_ref, basis_ref, residual_ref, split_ref, terms, landing):
    sources, height, _ = arrived_ref.shape
    width = height - 8
    for source in range(sources):
        columns = slice(source * CAP, (source + 1) * CAP)
        high, low = split_values(arrived_ref[source, :width, :])
        terms[:width, columns] = high
        terms[width : 2 * width, columns] = low
        extra = arrived_ref[source, width:, :]
        terms[2 * width :, columns] = split_extra(extra)
        landing[:, columns] = extra[1:2, :].astype(jnp.int32)
    targets = landing[...]
    for tile in range(ROWS_DEV // CAP):
        columns = slice(tile * CAP, (tile + 1) * CAP)
        total = join(pick(terms[...], targets, tile * CAP), width) + local_ref[:, columns]
        basis_ref[:, columns] = total[:width]
        residual_ref[:, columns] = total[width : width + 1]
    part = split_ref.shape[2]
    for index in range(split_ref.shape[0]):
        split_ref[index] = basis_ref[:, index * part : (index + 1) * part]


def gram_kernel(basis_ref, residual_ref, out_ref):
    basis = basis_ref[...]
    size = basis.shape[0]
    gram = dot_nt(basis, basis, HIGHEST)
    residual = jnp.broadcast_to(residual_ref[...], (8, basis.shape[1]))
    gradient = dot_nt(residual, basis, HIGHEST)[:1]
    row, column = iota((size, size), 0), iota((size, size), 1)
    gram = jnp.where((row == size - 1) & (column < size - 1), gradient, gram)
    turned = pltpu.roll(jnp.broadcast_to(gradient, (8, size)), 1, axis=1)[:1]
    out_ref[...] = jnp.where((row == size - 2) & (column == 0), turned, gram)


def total_kernel(parts_ref, out_ref):
    total = jnp.sum(parts_ref[...], axis=0)
    for index in range(out_ref.shape[0]):
        out_ref[index] = total


def inverse(matrix):
    size = matrix.shape[0]
    shape = (8, size)
    row, lane = iota(shape, 0), iota(shape, 1)

    def step(_, groups):
        panel = groups[0]
        columns = [jnp.broadcast_to(panel[:, j : j + 1], shape) for j in range(8)]
        work = jnp.where(lane < 8, (lane == row).astype(F32), panel)
        for i in range(8):
            here = row == i
            scale = 1.0 / jnp.broadcast_to(columns[i][i : i + 1], shape)
            factor = columns[i]
            moved = jnp.broadcast_to(work[i : i + 1], shape) * scale
            work = jnp.where(here, moved, work - factor * moved)
            for j in range(i + 1, 8):
                moved = jnp.broadcast_to(columns[j][i : i + 1], shape) * scale
                columns[j] = jnp.where(here, moved, columns[j] - factor * moved)
        spread = [jnp.broadcast_to(work[k : k + 1], shape) for k in range(8)]
        done = []
        for other in groups[1:]:
            out = jnp.where(lane < 8, 0.0, other)
            for k in range(8):
                out = out - jnp.broadcast_to(other[:, k : k + 1], shape) * spread[k]
            done.append(out)
        return tuple(pltpu.roll(x, size - 8, axis=1) for x in done + [work])

    groups = tuple(matrix[k : k + 8] for k in range(0, size, 8))
    return jnp.concatenate(lax.fori_loop(0, size // 8, step, groups), axis=0)


def solve_kernel(gram_ref, out_ref):
    size = gram_ref.shape[0]
    half = size // 2
    row, column = iota((half, half), 0), iota((half, half), 1)
    upper = row <= column

    def mirrored(block):
        block = jnp.where(upper, block, 0.0)
        return block + jnp.where(row == column, 0.0, block).T

    lane = iota((1, size), 1)
    last = jnp.sum(
        jnp.where(lane == 0, gram_ref[size - 2 : size - 1, :], 0.0), axis=1, keepdims=True
    )
    gradient = jnp.where(lane == size - 1, last, gram_ref[size - 1 : size, :])
    gradient = jnp.broadcast_to(gradient, (8, size))
    first = mirrored(gram_ref[:half, :half])
    cross = gram_ref[:half, half:]
    second = mirrored(gram_ref[half:, half:])
    first_inverse = inverse(first)
    carried = dot_nn(first_inverse, cross, HIGHEST)
    second_inverse = inverse(second - dot_tn(cross, carried, HIGHEST))

    def apply(top, bottom):
        low = dot_nt(bottom - dot_nn(top, carried, HIGHEST), second_inverse, HIGHEST)
        return dot_nt(top, first_inverse, HIGHEST) - dot_nt(low, carried, HIGHEST), low

    top, bottom = gradient[:, :half], gradient[:, half:]
    x_top, x_bottom = apply(top, bottom)
    off_top = top - dot_nn(x_top, first, HIGHEST) - dot_nt(x_bottom, cross, HIGHEST)
    off_bottom = bottom - dot_nn(x_top, cross, HIGHEST) - dot_nn(x_bottom, second, HIGHEST)
    more_top, more_bottom = apply(off_top, off_bottom)
    out_ref[:, :half] = -(x_top + more_top)[:1]
    out_ref[:, half:] = -(x_bottom + more_bottom)[:1]


VMEM = pl.BlockSpec(memory_space=pltpu.VMEM)
SMEM = pl.BlockSpec(memory_space=pltpu.SMEM)


def body(basis_panel, jacobian, neighbors, sample_rows, residual_parts):
    dom_count, col_count = lax.axis_size("dom"), lax.axis_size("col")
    col_index = lax.axis_index("col")
    width = basis_panel.shape[0]
    entries = sample_rows.shape[0]
    elements = neighbors.shape[0]
    node = jacobian.shape[1]
    size = width * col_count
    shape = jax.ShapeDtypeStruct
    local, send = pl.pallas_call(
        functools.partial(product_kernel, dom_count),
        out_shape=(shape((width + 8, ROWS_DEV), F32), shape((dom_count, width + 8, CAP), F32)),
        in_specs=[SMEM, SMEM, VMEM, VMEM, VMEM, VMEM],
        out_specs=(VMEM, VMEM),
        scratch_shapes=[
            pltpu.VMEM((elements, width, node), BF16),
            pltpu.VMEM((2 * width + 32, entries), BF16),
        ],
        name="products",
    )(
        lax.axis_index("dom").astype(jnp.int32).reshape(1),
        neighbors,
        basis_panel,
        jacobian,
        sample_rows.reshape(1, entries),
        residual_parts.reshape(1, entries),
    )
    arrived = lax.all_to_all(send, "dom", split_axis=0, concat_axis=0, tiled=True)
    part = ROWS_DEV // col_count
    jacobian_basis, sampled_residual, pieces = pl.pallas_call(
        assemble_kernel,
        out_shape=(
            shape((width, ROWS_DEV), F32),
            shape((1, ROWS_DEV), F32),
            shape((col_count, width, part), F32),
        ),
        in_specs=[VMEM, VMEM],
        out_specs=(VMEM, VMEM, VMEM),
        scratch_shapes=[
            pltpu.VMEM((2 * width + 32, dom_count * CAP), BF16),
            pltpu.VMEM((1, dom_count * CAP), jnp.int32),
        ],
        name="assemble",
    )(local, arrived)
    pieces = lax.all_to_all(pieces, "col", split_axis=0, concat_axis=0, tiled=True)
    own_residual = lax.dynamic_slice_in_dim(sampled_residual, col_index * part, part, axis=1)
    gram = pl.pallas_call(
        gram_kernel,
        out_shape=shape((size, size), F32),
        in_specs=[VMEM, VMEM],
        out_specs=VMEM,
        name="gram",
    )(pieces.reshape(size, part), own_residual)
    devices = dom_count * col_count
    chunk = (devices, size // devices, size) if size % devices == 0 else (devices, 1, size * size // devices)
    spread = lax.all_to_all(
        gram.reshape(chunk), ("dom", "col"), split_axis=0, concat_axis=0, tiled=True
    )
    summed = pl.pallas_call(
        total_kernel, out_shape=shape(chunk, F32), in_specs=[VMEM], out_specs=VMEM, name="total"
    )(spread)
    whole = lax.all_to_all(summed, ("dom", "col"), split_axis=0, concat_axis=0, tiled=True)
    full_step = pl.pallas_call(
        solve_kernel,
        out_shape=shape((1, size), F32),
        in_specs=[VMEM],
        out_specs=VMEM,
        name="solve",
    )(whole.reshape(size, size))
    reduced_step = lax.dynamic_slice_in_dim(full_step[0], col_index * width, width)
    return (jacobian_basis, sampled_residual[0], reduced_step)


def solution(mesh):
    placed = (P("col", "dom"), P(None, None, "dom"), P("dom", None), P("dom"), P("dom"))
    return jax.shard_map(
        body,
        mesh=mesh,
        in_specs=placed,
        out_specs=(P("col", "dom"), P("dom"), P("col")),
        check_vma=False,
    )
```

time: 270 us -> 101 us (0.37)
  other arithmetic: 107 us -> 0 us
  local copies, waits for them, and re-layouts: 53.5 us -> 5.24 us
  Pallas kernels: 0 us -> 40 us
  between operations: 16.2 us -> 0.66 us
  blocking collectives: 40.7 us -> 29.2 us
  waiting for transfers between devices: 28.1 us -> 17.9 us
  matrix products: 9.92 us -> 0 us
  starting transfers between devices: 13.6 us -> 7.85 us
    another operation x12 -> x0, other arithmetic: 56.8 us -> none  [the longest x7 34.7 us: body(): factor = jnp.linalg.cholesky(gram_matrix)]
    scatter-add x4 -> x0, other arithmetic: 47.9 us -> none  [the longest x1 13 us: body(): sampled_residual.at[landing].add(arrived_residual.reshape(-1), mode='drop')]
    pallas_call x0 -> x5, Pallas kernels: none -> 40 us  [the longest x1 16.6 us: body(): pl.pallas_call(functools.partial(product_kernel, dom_count), out_shape=(s...]
    all_to_all x0 -> x2, blocking collectives: none -> 29.2 us  [the longest x1 15.7 us: body(): lax.all_to_all(send, 'dom', split_axis=0, concat_axis=0, tiled=True)]
    psum x1 -> x0, waiting for transfers between devices: 28.1 us -> none  [body(): gram_panel, gradient_panel = lax.psum((gram_panel, gradient_panel), 'dom')]
    scatter x3 -> x0, local copies, waits for them, and re-layouts: 23.2 us -> none  [the longest x1 8.77 us: body(): send_residual = jnp.zeros((dom_count * CAP,), jnp.float32).at[target_slot...]
    all_to_all x3 -> x2, waiting for transfers between devices: 0.01 us -> 17.9 us  [the longest x1 10.2 us: body(): lax.all_to_all(summed, ('dom', 'col'), split_axis=0, concat_axis=0, tiled...]
    psum x1 -> x0, blocking collectives: 14.4 us -> none  [body(): gram_panel, gradient_panel = lax.psum((gram_panel, gradient_panel), 'dom')]
  transfers between devices with their start and end apart: 5 -> 2, of which waited for: 1 -> 2; matrix products, arithmetic and copies ran while one was open for 30% -> 1% of each run, Pallas kernels for 0% -> 0%
where the time goes in v1:
time: 101 us
  Pallas kernels  40 us (40%)
  blocking collectives  29.2 us (29%)
  waiting for transfers between devices  17.9 us (18%)
  starting transfers between devices  7.85 us (8%)
  local copies, waits for them, and re-layouts  5.24 us (5%)
    pallas_call x1, Pallas kernels, body(): pl.pallas_call(functools.partial(product_kernel, dom_count), out_shape=(s...  16.6 us
    pallas_call x1, Pallas kernels, body(): pl.pallas_call(solve_kernel, out_shape=shape((1, size), F32), in_specs=[V...  16 us
    all_to_all x1, blocking collectives, body(): lax.all_to_all(send, 'dom', split_axis=0, concat_axis=0, tiled=True)  15.7 us
    all_to_all x1, blocking collectives, body(): lax.all_to_all(gram.reshape(chunk), ('dom', 'col'), split_axis=0, concat_...  13.5 us
    all_to_all x1, waiting for transfers between devices, body(): lax.all_to_all(summed, ('dom', 'col'), split_axis=0, concat_axis=0, tiled...  10.2 us
    all_to_all x1, waiting for transfers between devices, body(): lax.all_to_all(pieces, 'col', split_axis=0, concat_axis=0, tiled=True)  7.63 us
    all_to_all x1, starting transfers between devices, body(): lax.all_to_all(pieces, 'col', split_axis=0, concat_axis=0, tiled=True)  5.22 us
    pallas_call x1, Pallas kernels, body(): pl.pallas_call(assemble_kernel, out_shape=(shape((width, ROWS_DEV), F32),...  3.48 us
  transfers between devices with their start and end apart: 2, of which 2 were waited for; matrix products, arithmetic and copies ran while one was open for 1% of the time, Pallas kernels for 0%

profile of v1, /device:TPU:0, one launch (start us, length us, event | category | flops | bytes accessed | tf_op | source)
XLA Modules:
  0.0 100.8 jit_solution(14874533751690641026)
XLA Ops:
  0.6 1.4 %copy.8.links_ref = s32[64,2]{1,0:T(8,128)} copy(s32[64,2]{0,1:T(2,128)} %param.7) | data formatting | bytes 1024 | tf_op args[2]
  2.0 16.6 %products.1 = (f32[72,1024]{1,0:T(8,128)}, f32[8,72,256]{2,1,0:T(8,128)}) custom-call(s32[1]{0:T(128)} %bitcast.self_ref, s32[64,2]{1,0:T(8,128)} %copy.8.links_ref, bf16[64,20480]{1,0:T(8,128)(2,1)} %panel_ref.1, bf16[2,320,2048]{2,1,0:T(8,128)(2,1)} %blocks_ref.1, s32[1,2048]{1,0:T(1,128)} %bitcast.12, f32[1,2048]{1,0:T(1,128)} %bitcast.13), custom_call_target="tpu_custom_call" | custom-call | tf_op jit(solution)/shard_map/products/pallas_call | solution.py:253
  18.6 15.7 %all_to_all.20.arrived_ref = f32[8,72,256]{2,1,0:T(8,128)} all-to-all(f32[8,72,256]{2,1,0:T(8,128)} %get-tuple-element.9), channel_id=1, replica_groups=mesh['dom'=8,'col'=4] {'dom'}, dimensions={0} | all-to-all | bytes 1179648 | tf_op jit(solution)/shard_map/all_to_all | solution.py:271
  34.3 3.5 %assemble.1 = (f32[64,1024]{1,0:T(8,128)}, f32[1,1024]{1,0:T(1,128)}, f32[4,64,256]{2,1,0:T(8,128)}) custom-call(f32[72,1024]{1,0:T(8,128)} %get-tuple-element.8.local_ref, f32[8,72,256]{2,1,0:T(8,128)} %all_to_all.20.arrived_ref), custom_call_target="tpu_custom_call" | custom-call | tf_op jit(solution)/shard_map/assemble/pallas_call | solution.py:273
  37.8 5.2 %all-to-all-start.1 = ((f32[4,64,256]{2,1,0:T(8,128)}), f32[4,64,256]{2,1,0:T(8,128)S(1)}, u32[]{:S(2)}, u32[]{:S(2)}) async-start(f32[4,64,256]{2,1,0:T(8,128)} %get-tuple-element.12), calls=%async_computation.1 | async-start | bytes 524288 | tf_op jit(solution)/shard_map/all_to_all | solution.py:288
  43.0 1.2 %constant_dynamic-slice_fusion.residual_ref = f32[1,256]{1,0:T(1,128)} fusion(f32[1,1024]{1,0:T(1,128)} %get-tuple-element.11, s32[]{:T(128)S(6)} %select_n.6), kind=kLoop, calls=%fused_computation.1 | loop fusion | bytes 2052 | tf_op jit(solution)/shard_map/dynamic_slice | solution.py:289
  44.2 7.6 %all-to-all-done.1 = f32[4,64,256]{2,1,0:T(8,128)S(1)} async-done(((f32[4,64,256]{2,1,0:T(8,128)}), f32[4,64,256]{2,1,0:T(8,128)S(1)}, u32[]{:S(2)}, u32[]{:S(2)}) %all-to-all-start.1) | async-done | bytes 262176 | tf_op jit(solution)/shard_map/all_to_all | solution.py:288
  51.9 0.0 copy-start
  51.9 0.7 copy-done
  52.6 2.2 %gram.1 = f32[256,256]{1,0:T(8,128)} custom-call(f32[256,256]{1,0:T(8,128)} %bitcast.9, f32[1,256]{1,0:T(1,128)} %constant_dynamic-slice_fusion.residual_ref), custom_call_target="tpu_custom_call" | custom-call | tf_op jit(solution)/shard_map/gram/pallas_call | solution.py:290
  54.8 13.5 %all_to_all.21.parts_ref = f32[32,8,256]{2,1,0:T(8,128)} all-to-all(f32[32,8,256]{2,1,0:T(8,128)} %bitcast.11), channel_id=1, replica_groups=mesh['dom'=8,'col'=4] {'dom','col'}, dimensions={0} | all-to-all | bytes 524288 | tf_op jit(solution)/shard_map/all_to_all | solution.py:299
  68.3 1.7 %total.1 = f32[32,8,256]{2,1,0:T(8,128)} custom-call(f32[32,8,256]{2,1,0:T(8,128)} %all_to_all.21.parts_ref), custom_call_target="tpu_custom_call" | custom-call | tf_op jit(solution)/shard_map/total/pallas_call | solution.py:302
  70.0 2.6 %all-to-all-start.3 = ((f32[32,8,256]{2,1,0:T(8,128)}), f32[32,8,256]{2,1,0:T(8,128)S(1)}, u32[]{:S(2)}, u32[]{:S(2)}) async-start(f32[32,8,256]{2,1,0:T(8,128)} %total.1), calls=%async_computation.3 | async-start | bytes 524288 | tf_op jit(solution)/shard_map/all_to_all | solution.py:305
  72.7 10.2 %all-to-all-done.3 = f32[32,8,256]{2,1,0:T(8,128)S(1)} async-done(((f32[32,8,256]{2,1,0:T(8,128)}), f32[32,8,256]{2,1,0:T(8,128)S(1)}, u32[]{:S(2)}, u32[]{:S(2)}) %all-to-all-start.3) | async-done | bytes 262176 | tf_op jit(solution)/shard_map/all_to_all | solution.py:305
  82.9 0.0 copy-start.1
  82.9 0.7 copy-done.1
  83.6 16.0 %solve.1 = f32[1,256]{1,0:T(1,128)} custom-call(f32[256,256]{1,0:T(8,128)} %bitcast.10), custom_call_target="tpu_custom_call" | custom-call | tf_op jit(solution)/shard_map/solve/pallas_call | solution.py:306
  99.6 1.2 %dynamic-slice_bitcast_fusion = f32[64]{0:T(128)} fusion(f32[1,256]{1,0:T(1,128)} %solve.1, s32[]{:T(128)S(6)} %select_n.7), kind=kLoop, calls=%fused_computation | loop fusion | bytes 516 | tf_op jit(solution)/shard_map/dynamic_slice | solution.py:313
Async XLA Ops:
  37.8 14.1 %all-to-all-start.1 = ((f32[4,64,256]{2,1,0:T(8,128)}), f32[4,64,256]{2,1,0:T(8,128)S(1)}, u32[]{:S(2)}, u32[]{:S(2)}) async-start(f32[4,64,256]{2,1,0:T(8,128)} %get-tuple-element.12), calls=%async_computation.1 | async-start | bytes 524288 | tf_op jit(solution)/shard_map/all_to_all | solution.py:288
  51.9 0.7 copy-start
  70.0 12.9 %all-to-all-start.3 = ((f32[32,8,256]{2,1,0:T(8,128)}), f32[32,8,256]{2,1,0:T(8,128)S(1)}, u32[]{:S(2)}, u32[]{:S(2)}) async-start(f32[32,8,256]{2,1,0:T(8,128)} %total.1), calls=%async_computation.3 | async-start | bytes 524288 | tf_op jit(solution)/shard_map/all_to_all | solution.py:305
  82.9 0.7 copy-start.1

commit v2 on v1

--- a/solution.py
+++ b/solution.py
@@ -9,6 +9,7 @@
 
 ROWS_DEV = 1024
 CAP = 256
+REACH_MOST = 8
 LANES = 128
 HIGHEST = lax.Precision.HIGHEST
 F32 = jnp.float32
@@ -61,15 +62,62 @@
     return dot_nt(terms, (spots == targets).astype(F32).astype(BF16))
 
 
-def product_kernel(
-    dom_count, self_ref, links_ref, panel_ref, blocks_ref, rows_ref, parts_ref,
-    local_ref, send_ref, panels, terms,
+def fold(value, count):
+    return jnp.where(value >= count, value - count, value)
+
+
+def step_kernel(
+    dom_count, col_count, reach, links_ref, panel_ref, blocks_ref, rows_ref, parts_ref,
+    basis_ref, residual_ref, gram_ref,
+    panels, terms, send, arrived, local, terms_in, landing, pieces, others, parts, sums, total,
+    whole, dom_sems, col_sems, sum_sems, all_sems,
 ):
+    dom, col = lax.axis_index("dom"), lax.axis_index("col")
+    devices = dom_count * col_count
+    me = dom * col_count + col
     width = panel_ref.shape[0]
     coupled_count, node, entries = blocks_ref.shape
     elements = links_ref.shape[0]
     rs = entries // elements
     group = LANES // rs
+    part = ROWS_DEV // col_count
+    size = width * col_count
+
+    def remote(source, target, sems, index, device):
+        return pltpu.make_async_remote_copy(
+            src_ref=source,
+            dst_ref=target,
+            send_sem=sems.at[0, index],
+            recv_sem=sems.at[1, index],
+            device_id=device,
+            device_id_type=pl.DeviceIdType.MESH,
+        )
+
+    def device_at(offset):
+        index = fold(me + offset, devices)
+        return index, (index // col_count, index % col_count)
+
+    def dom_copy(o):
+        return remote(send.at[o - 1], arrived.at[o - 1], dom_sems, o - 1, (fold(dom + o, dom_count), col))
+
+    def col_copy(o):
+        there = fold(col + o, col_count)
+        return remote(pieces.at[there], others.at[col], col_sems, o - 1, (dom, there))
+
+    def sum_copy(o):
+        index, device = device_at(o)
+        return remote(parts.at[index], sums.at[o - 1], sum_sems, o - 1, device)
+
+    def all_copy(o):
+        _, device = device_at(o)
+        return remote(total, whole.at[me], all_sems, o - 1, device)
+
+    barrier = pltpu.get_barrier_semaphore()
+
+    @pl.loop(1, devices)
+    def _(o):
+        _, device = device_at(o)
+        pl.semaphore_signal(barrier, inc=1, device_id=device, device_id_type=pl.DeviceIdType.MESH)
 
     @pl.loop(0, elements // 2)
     def _(pair):
@@ -82,20 +130,19 @@
     @pl.loop(0, elements // group)
     def _(block):
         columns = pl.ds(pl.multiple_of(block * LANES, LANES), LANES)
-        total = jnp.zeros((group * width, LANES), F32)
+        found = jnp.zeros((group * width, LANES), F32)
         for coupled in range(coupled_count):
             picked = jnp.concatenate(
                 [panels[links_ref[block * group + q, coupled]] for q in range(group)], axis=0
             )
-            total = total + dot_nn(picked, blocks_ref[coupled, :, columns])
-        out = total[:width]
+            found = found + dot_nn(picked, blocks_ref[coupled, :, columns])
+        out = found[:width]
         for q in range(1, group):
-            out = jnp.where(lane_element == q, total[q * width : (q + 1) * width], out)
+            out = jnp.where(lane_element == q, found[q * width : (q + 1) * width], out)
         high, low = split_values(out)
         terms[:width, columns] = high
         terms[width : 2 * width, columns] = low
 
-    own = self_ref[0]
     shift = ROWS_DEV.bit_length() - 1
     match_rows = max(16, dom_count)
     before = (iota((LANES, LANES), 0) < iota((LANES, LANES), 1)).astype(F32).astype(BF16)
@@ -103,14 +150,16 @@
     targets = []
     for start in range(0, entries, LANES):
         rows = rows_ref[:, start : start + LANES]
-        owner = rows >> shift
+        offset = fold((rows >> shift) - dom + dom_count, dom_count)
         local_row = rows & (ROWS_DEV - 1)
-        matches = (iota((match_rows, LANES), 0) == owner).astype(F32)
+        matches = (iota((match_rows, LANES), 0) == offset).astype(F32)
         ranks = jnp.sum(
             matches * (dot_nn(matches.astype(BF16), before) + carry), axis=0, keepdims=True
         ).astype(jnp.int32)
         carry = carry + jnp.sum(matches, axis=1, keepdims=True)
-        targets.append(jnp.where(owner == own, local_row, ROWS_DEV + owner * CAP + ranks))
+        targets.append(
+            jnp.where(offset == 0, local_row, ROWS_DEV + (offset - 1) * CAP + ranks)
+        )
     targets = jnp.concatenate(targets, axis=1)
 
     row_values = (rows_ref[...] & (ROWS_DEV - 1)).astype(F32)
@@ -118,56 +167,110 @@
     extra = jnp.where(which == 0, parts_ref[...], jnp.where(which == 1, row_values, 0.0))
     terms[2 * width :, :] = split_extra(extra)
 
+    pl.semaphore_wait(barrier, devices - 1)
+
+    @pl.loop(1, reach + 1)
+    def _(o):
+        send[o - 1] = join(pick(terms[...], targets, ROWS_DEV + (o - 1) * CAP), width)
+        dom_copy(o).start()
+
     @pl.loop(0, ROWS_DEV // CAP)
     def _(tile):
         base = tile * CAP
-        local_ref[:, pl.ds(pl.multiple_of(base, CAP), CAP)] = join(
+        local[:, pl.ds(pl.multiple_of(base, CAP), CAP)] = join(
             pick(terms[...], targets, base), width
         )
 
-    @pl.loop(0, dom_count)
-    def _(owner):
-        send_ref[owner] = join(pick(terms[...], targets, ROWS_DEV + owner * CAP), width)
-
-
-def assemble_kernel(local_ref, arrived_ref, basis_ref, residual_ref, split_ref, terms, landing):
-    sources, height, _ = arrived_ref.shape
-    width = height - 8
-    for source in range(sources):
-        columns = slice(source * CAP, (source + 1) * CAP)
-        high, low = split_values(arrived_ref[source, :width, :])
-        terms[:width, columns] = high
-        terms[width : 2 * width, columns] = low
-        extra = arrived_ref[source, width:, :]
-        terms[2 * width :, columns] = split_extra(extra)
+    for o in range(1, reach + 1):
+        dom_copy(o).wait_recv()
+        columns = slice((o - 1) * CAP, o * CAP)
+        high, low = split_values(arrived[o - 1, :width, :])
+        terms_in[:width, columns] = high
+        terms_in[width : 2 * width, columns] = low
+        extra = arrived[o - 1, width:, :]
+        terms_in[2 * width :, columns] = split_extra(extra)
         landing[:, columns] = extra[1:2, :].astype(jnp.int32)
     targets = landing[...]
-    for tile in range(ROWS_DEV // CAP):
-        columns = slice(tile * CAP, (tile + 1) * CAP)
-        total = join(pick(terms[...], targets, tile * CAP), width) + local_ref[:, columns]
-        basis_ref[:, columns] = total[:width]
-        residual_ref[:, columns] = total[width : width + 1]
-    part = split_ref.shape[2]
-    for index in range(split_ref.shape[0]):
-        split_ref[index] = basis_ref[:, index * part : (index + 1) * part]
-
-
-def gram_kernel(basis_ref, residual_ref, out_ref):
-    basis = basis_ref[...]
-    size = basis.shape[0]
+
+    def assemble(base):
+        columns = pl.ds(pl.multiple_of(base, CAP), CAP)
+        found = join(pick(terms_in[...], targets, base), width) + local[:, columns]
+        basis_ref[:, columns] = found[:width]
+        residual_ref[:, columns] = found[width : width + 1]
+        return found
+
+    if part == CAP:
+
+        @pl.loop(1, col_count)
+        def _(o):
+            there = fold(col + o, col_count)
+            pieces[there] = assemble(there * part)[:width]
+            col_copy(o).start()
+
+        found = assemble(col * part)
+        others[col] = found[:width]
+        own_residual = found[width : width + 1]
+    else:
+        for tile in range(ROWS_DEV // CAP):
+            assemble(tile * CAP)
+        own_residual = jnp.zeros((1, part), F32)
+        for index in range(col_count):
+            columns = slice(index * part, (index + 1) * part)
+            pieces[index] = basis_ref[:, columns]
+            own_residual = own_residual + jnp.where(index == col, residual_ref[:, columns], 0.0)
+        for o in range(1, col_count):
+            col_copy(o).start()
+        others[col] = pieces[col]
+    for o in range(1, col_count):
+        col_copy(o).wait_recv()
+
+    basis = others[...].reshape(size, part)
     gram = dot_nt(basis, basis, HIGHEST)
-    residual = jnp.broadcast_to(residual_ref[...], (8, basis.shape[1]))
-    gradient = dot_nt(residual, basis, HIGHEST)[:1]
+    gradient = dot_nt(jnp.broadcast_to(own_residual, (8, part)), basis, HIGHEST)[:1]
     row, column = iota((size, size), 0), iota((size, size), 1)
     gram = jnp.where((row == size - 1) & (column < size - 1), gradient, gram)
     turned = pltpu.roll(jnp.broadcast_to(gradient, (8, size)), 1, axis=1)[:1]
-    out_ref[...] = jnp.where((row == size - 2) & (column == 0), turned, gram)
-
-
-def total_kernel(parts_ref, out_ref):
-    total = jnp.sum(parts_ref[...], axis=0)
-    for index in range(out_ref.shape[0]):
-        out_ref[index] = total
+    gram = jnp.where((row == size - 2) & (column == 0), turned, gram)
+    count, height, span = parts.shape
+    if span == size:
+        for index in range(count):
+            parts[index] = gram[index * height : (index + 1) * height]
+    else:
+        for index in range(count):
+            start = index * span % size
+            parts[index] = gram[index * span // size][None, start : start + span]
+
+    @pl.loop(1, devices)
+    def _(o):
+        sum_copy(o).start()
+
+    @pl.loop(1, devices)
+    def _(o):
+        sum_copy(o).wait_recv()
+
+    mine = jnp.sum(sums[...], axis=0) + parts[me]
+    total[...] = mine
+
+    @pl.loop(1, devices)
+    def _(o):
+        all_copy(o).start()
+
+    whole[me] = mine
+
+    @pl.loop(1, devices)
+    def _(o):
+        all_copy(o).wait_recv()
+
+    gram_ref[...] = whole[...]
+    for o in range(1, reach + 1):
+        dom_copy(o).wait_send()
+    for o in range(1, col_count):
+        col_copy(o).wait_send()
+
+    @pl.loop(1, devices)
+    def _(o):
+        sum_copy(o).wait_send()
+        all_copy(o).wait_send()
 
 
 def inverse(matrix):
@@ -250,59 +353,48 @@
     node = jacobian.shape[1]
     size = width * col_count
     shape = jax.ShapeDtypeStruct
-    local, send = pl.pallas_call(
-        functools.partial(product_kernel, dom_count),
-        out_shape=(shape((width + 8, ROWS_DEV), F32), shape((dom_count, width + 8, CAP), F32)),
-        in_specs=[SMEM, SMEM, VMEM, VMEM, VMEM, VMEM],
-        out_specs=(VMEM, VMEM),
+    reach = min(dom_count - 1, REACH_MOST)
+    part = ROWS_DEV // col_count
+    devices = dom_count * col_count
+    if size % devices == 0:
+        chunk = (devices, size // devices, size)
+    else:
+        chunk = (devices, 1, size * size // devices)
+    jacobian_basis, sampled_residual, whole = pl.pallas_call(
+        functools.partial(step_kernel, dom_count, col_count, reach),
+        out_shape=(
+            shape((width, ROWS_DEV), F32), shape((1, ROWS_DEV), F32), shape(chunk, F32)
+        ),
+        in_specs=[SMEM, VMEM, VMEM, VMEM, VMEM],
+        out_specs=(VMEM, VMEM, VMEM),
         scratch_shapes=[
             pltpu.VMEM((elements, width, node), BF16),
             pltpu.VMEM((2 * width + 32, entries), BF16),
+            pltpu.VMEM((reach, width + 8, CAP), F32),
+            pltpu.VMEM((reach, width + 8, CAP), F32),
+            pltpu.VMEM((width + 8, ROWS_DEV), F32),
+            pltpu.VMEM((2 * width + 32, reach * CAP), BF16),
+            pltpu.VMEM((1, reach * CAP), jnp.int32),
+            pltpu.VMEM((col_count, width, part), F32),
+            pltpu.VMEM((col_count, width, part), F32),
+            pltpu.VMEM(chunk, F32),
+            pltpu.VMEM((devices - 1,) + chunk[1:], F32),
+            pltpu.VMEM(chunk[1:], F32),
+            pltpu.VMEM(chunk, F32),
+            pltpu.SemaphoreType.DMA((2, reach)),
+            pltpu.SemaphoreType.DMA((2, col_count - 1)),
+            pltpu.SemaphoreType.DMA((2, devices - 1)),
+            pltpu.SemaphoreType.DMA((2, devices - 1)),
         ],
-        name="products",
+        compiler_params=pltpu.CompilerParams(collective_id=0, has_side_effects=True),
+        name="step",
     )(
-        lax.axis_index("dom").astype(jnp.int32).reshape(1),
         neighbors,
         basis_panel,
         jacobian,
         sample_rows.reshape(1, entries),
         residual_parts.reshape(1, entries),
     )
-    arrived = lax.all_to_all(send, "dom", split_axis=0, concat_axis=0, tiled=True)
-    part = ROWS_DEV // col_count
-    jacobian_basis, sampled_residual, pieces = pl.pallas_call(
-        assemble_kernel,
-        out_shape=(
-            shape((width, ROWS_DEV), F32),
-            shape((1, ROWS_DEV), F32),
-            shape((col_count, width, part), F32),
-        ),
-        in_specs=[VMEM, VMEM],
-        out_specs=(VMEM, VMEM, VMEM),
-        scratch_shapes=[
-            pltpu.VMEM((2 * width + 32, dom_count * CAP), BF16),
-            pltpu.VMEM((1, dom_count * CAP), jnp.int32),
-        ],
-        name="assemble",
-    )(local, arrived)
-    pieces = lax.all_to_all(pieces, "col", split_axis=0, concat_axis=0, tiled=True)
-    own_residual = lax.dynamic_slice_in_dim(sampled_residual, col_index * part, part, axis=1)
-    gram = pl.pallas_call(
-        gram_kernel,
-        out_shape=shape((size, size), F32),
-        in_specs=[VMEM, VMEM],
-        out_specs=VMEM,
-        name="gram",
-    )(pieces.reshape(size, part), own_residual)
-    devices = dom_count * col_count
-    chunk = (devices, size // devices, size) if size % devices == 0 else (devices, 1, size * size // devices)
-    spread = lax.all_to_all(
-        gram.reshape(chunk), ("dom", "col"), split_axis=0, concat_axis=0, tiled=True
-    )
-    summed = pl.pallas_call(
-        total_kernel, out_shape=shape(chunk, F32), in_specs=[VMEM], out_specs=VMEM, name="total"
-    )(spread)
-    whole = lax.all_to_all(summed, ("dom", "col"), split_axis=0, concat_axis=0, tiled=True)
     full_step = pl.pallas_call(
         solve_kernel,
         out_shape=shape((1, size), F32),

time: 101 us -> 72.9 us (0.72)
  blocking collectives: 29.2 us -> 0 us
  Pallas kernels: 40 us -> 66.5 us
  waiting for transfers between devices: 17.9 us -> 0 us
  starting transfers between devices: 7.85 us -> 0 us
    all_to_all x2 -> x0, blocking collectives: 29.2 us -> none  [the longest x1 15.7 us: body(): lax.all_to_all(send, 'dom', split_axis=0, concat_axis=0, tiled=True)]
    pallas_call x4 -> x1, Pallas kernels: 24 us -> 50.5 us  [body(): pl.pallas_call(functools.partial(step_kernel, dom_count, col_count, reach...]
    all_to_all x2 -> x0, waiting for transfers between devices: 17.9 us -> none  [the longest x1 10.2 us: body(): lax.all_to_all(summed, ('dom', 'col'), split_axis=0, concat_axis=0, tiled...]
    all_to_all x2 -> x0, starting transfers between devices: 7.85 us -> none  [the longest x1 5.22 us: body(): lax.all_to_all(pieces, 'col', split_axis=0, concat_axis=0, tiled=True)]
    unnamed x5 -> x3, local copies, waits for them, and re-layouts: 2.78 us -> 4.32 us
    dynamic_slice x1 -> x0, local copies, waits for them, and re-layouts: 1.21 us -> none  [body(): lax.dynamic_slice_in_dim(sampled_residual, col_index * part, part, axis=1)]
  transfers between devices with their start and end apart: 2 -> 0, of which waited for: 2 -> 0; matrix products, arithmetic and copies ran while one was open for 1% -> 0% of each run, Pallas kernels for 0% -> 0%
where the time goes in v2:
time: 72.9 us; the launch traced here: 72.7 us
  Pallas kernels  66.5 us (91%)
  local copies, waits for them, and re-layouts  5.55 us (8%)
    pallas_call x1, Pallas kernels, body(): pl.pallas_call(functools.partial(step_kernel, dom_count, col_count, reach...  50.5 us
    pallas_call x1, Pallas kernels, body(): pl.pallas_call(solve_kernel, out_shape=shape((1, size), F32), in_specs=[V...  16 us
    unnamed x3, local copies, waits for them, and re-layouts  4.32 us

profile of v2, /device:TPU:0, one launch (start us, length us, event | category | flops | bytes accessed | tf_op | source)
XLA Modules:
  0.0 72.7 jit_solution(8571193690382854498)
XLA Ops:
  0.6 1.4 %copy.8.links_ref = s32[64,2]{1,0:T(8,128)} copy(s32[64,2]{0,1:T(2,128)} %param.7) | data formatting | bytes 1024 | tf_op args[2]
  2.0 50.5 %step.1 = (f32[64,1024]{1,0:T(8,128)}, f32[1,1024]{1,0:T(1,128)}, f32[32,8,256]{2,1,0:T(8,128)}) custom-call(s32[64,2]{1,0:T(8,128)} %copy.8.links_ref, bf16[64,20480]{1,0:T(8,128)(2,1)} %panel_ref.1, bf16[2,320,2048]{2,1,0:T(8,128)(2,1)} %blocks_ref.1, s32[1,2048]{1,0:T(1,128)} %bitcast.7, f32[1,2048]{1,0:T(1,128)} %bitcast.8), custom_call_target="tpu_custom_call" | custom-call | tf_op jit(solution)/shard_map/step/pallas_call | solution.py:363
  52.6 16.0 %solve.1 = f32[1,256]{1,0:T(1,128)} custom-call(f32[256,256]{1,0:T(8,128)} %bitcast.6), custom_call_target="tpu_custom_call" | custom-call | tf_op jit(solution)/shard_map/solve/pallas_call | solution.py:398
  68.5 1.2 %dynamic-slice_bitcast_fusion = f32[64]{0:T(128)} fusion(f32[1,256]{1,0:T(1,128)} %solve.1, s32[]{:T(128)S(6)} %select_n.3), kind=kLoop, calls=%fused_computation | loop fusion | bytes 516 | tf_op jit(solution)/shard_map/dynamic_slice | solution.py:405
  69.8 1.7 %copy.11 = f32[64,1024]{1,0:T(8,128)} copy(f32[64,1024]{1,0:T(8,128)} %get-tuple-element.12) | data formatting | bytes 524288
  71.4 1.3 %copy.12 = f32[1024]{0:T(1024)} copy(f32[1024]{0:T(1024)} %bitcast.9) | data formatting | bytes 8192

commit v3 on v2

--- a/solution.py
+++ b/solution.py
@@ -67,9 +67,9 @@
 
 
 def step_kernel(
-    dom_count, col_count, reach, links_ref, panel_ref, blocks_ref, rows_ref, parts_ref,
+    dom_count, col_count, reach, links_ref, panel_hbm, blocks_hbm, rows_ref, parts_ref,
     basis_ref, residual_ref, gram_ref,
-    panels, terms, send, arrived, local, terms_in, landing, pieces, others, parts, sums, total,
+    panel_ref, blocks_ref, load_sems, panels, terms, send, arrived, local, terms_in, landing, pieces, others, parts, sums, total,
     whole, dom_sems, col_sems, sum_sems, all_sems,
 ):
     dom, col = lax.axis_index("dom"), lax.axis_index("col")
@@ -77,7 +77,7 @@
     me = dom * col_count + col
     width = panel_ref.shape[0]
     coupled_count, node, entries = blocks_ref.shape
-    elements = links_ref.shape[0]
+    elements = links_ref.shape[1]
     rs = entries // elements
     group = LANES // rs
     part = ROWS_DEV // col_count
@@ -112,36 +112,16 @@
         _, device = device_at(o)
         return remote(total, whole.at[me], all_sems, o - 1, device)
 
+    panel_load = pltpu.make_async_copy(panel_hbm, panel_ref, load_sems.at[0])
+    blocks_load = pltpu.make_async_copy(blocks_hbm, blocks_ref, load_sems.at[1])
+    panel_load.start()
+    blocks_load.start()
     barrier = pltpu.get_barrier_semaphore()
 
     @pl.loop(1, devices)
     def _(o):
         _, device = device_at(o)
         pl.semaphore_signal(barrier, inc=1, device_id=device, device_id_type=pl.DeviceIdType.MESH)
-
-    @pl.loop(0, elements // 2)
-    def _(pair):
-        window = panel_ref[:, pl.ds(pl.multiple_of(pair * 2 * node, LANES), 2 * node)]
-        panels[2 * pair] = window[:, :node]
-        panels[2 * pair + 1] = window[:, node:]
-
-    lane_element = iota((width, LANES), 1) // rs
-
-    @pl.loop(0, elements // group)
-    def _(block):
-        columns = pl.ds(pl.multiple_of(block * LANES, LANES), LANES)
-        found = jnp.zeros((group * width, LANES), F32)
-        for coupled in range(coupled_count):
-            picked = jnp.concatenate(
-                [panels[links_ref[block * group + q, coupled]] for q in range(group)], axis=0
-            )
-            found = found + dot_nn(picked, blocks_ref[coupled, :, columns])
-        out = found[:width]
-        for q in range(1, group):
-            out = jnp.where(lane_element == q, found[q * width : (q + 1) * width], out)
-        high, low = split_values(out)
-        terms[:width, columns] = high
-        terms[width : 2 * width, columns] = low
 
     shift = ROWS_DEV.bit_length() - 1
     match_rows = max(16, dom_count)
@@ -166,6 +146,34 @@
     which = iota((8, entries), 0)
     extra = jnp.where(which == 0, parts_ref[...], jnp.where(which == 1, row_values, 0.0))
     terms[2 * width :, :] = split_extra(extra)
+
+    panel_load.wait()
+
+    @pl.loop(0, elements // 2)
+    def _(pair):
+        window = panel_ref[:, pl.ds(pl.multiple_of(pair * 2 * node, LANES), 2 * node)]
+        panels[2 * pair] = window[:, :node]
+        panels[2 * pair + 1] = window[:, node:]
+
+    lane_element = iota((width, LANES), 1) // rs
+
+    blocks_load.wait()
+
+    @pl.loop(0, elements // group)
+    def _(block):
+        columns = pl.ds(pl.multiple_of(block * LANES, LANES), LANES)
+        found = jnp.zeros((group * width, LANES), F32)
+        for coupled in range(coupled_count):
+            picked = jnp.concatenate(
+                [panels[links_ref[coupled, block * group + q]] for q in range(group)], axis=0
+            )
+            found = found + dot_nn(picked, blocks_ref[coupled, :, columns])
+        out = found[:width]
+        for q in range(1, group):
+            out = jnp.where(lane_element == q, found[q * width : (q + 1) * width], out)
+        high, low = split_values(out)
+        terms[:width, columns] = high
+        terms[width : 2 * width, columns] = low
 
     pl.semaphore_wait(barrier, devices - 1)
 
@@ -301,10 +309,14 @@
         return tuple(pltpu.roll(x, size - 8, axis=1) for x in done + [work])
 
     groups = tuple(matrix[k : k + 8] for k in range(0, size, 8))
-    return jnp.concatenate(lax.fori_loop(0, size // 8, step, groups), axis=0)
-
-
-def solve_kernel(gram_ref, out_ref):
+    return jnp.concatenate(lax.fori_loop(0, size // 8, step, groups, unroll=2), axis=0)
+
+
+def solve_kernel(
+    col_ref, gram_ref, basis_ref, residual_ref, out_ref, basis_out_ref, residual_out_ref
+):
+    basis_out_ref[...] = basis_ref[...]
+    residual_out_ref[...] = residual_ref[...]
     size = gram_ref.shape[0]
     half = size // 2
     row, column = iota((half, half), 0), iota((half, half), 1)
@@ -336,12 +348,17 @@
     off_top = top - dot_nn(x_top, first, HIGHEST) - dot_nt(x_bottom, cross, HIGHEST)
     off_bottom = bottom - dot_nn(x_top, cross, HIGHEST) - dot_nn(x_bottom, second, HIGHEST)
     more_top, more_bottom = apply(off_top, off_bottom)
-    out_ref[:, :half] = -(x_top + more_top)[:1]
-    out_ref[:, half:] = -(x_bottom + more_bottom)[:1]
+    full = -jnp.concatenate([x_top + more_top, x_bottom + more_bottom], axis=1)[:1]
+    width = out_ref.shape[1]
+    out = jnp.zeros((1, width), F32)
+    for index in range(size // width):
+        out = jnp.where(col_ref[0] == index, full[:, index * width : (index + 1) * width], out)
+    out_ref[...] = out
 
 
 VMEM = pl.BlockSpec(memory_space=pltpu.VMEM)
 SMEM = pl.BlockSpec(memory_space=pltpu.SMEM)
+ANY = pl.BlockSpec(memory_space=pl.ANY)
 
 
 def body(basis_panel, jacobian, neighbors, sample_rows, residual_parts):
@@ -365,9 +382,12 @@
         out_shape=(
             shape((width, ROWS_DEV), F32), shape((1, ROWS_DEV), F32), shape(chunk, F32)
         ),
-        in_specs=[SMEM, VMEM, VMEM, VMEM, VMEM],
+        in_specs=[SMEM, ANY, ANY, VMEM, VMEM],
         out_specs=(VMEM, VMEM, VMEM),
         scratch_shapes=[
+            pltpu.VMEM(basis_panel.shape, BF16),
+            pltpu.VMEM(jacobian.shape, BF16),
+            pltpu.SemaphoreType.DMA((2,)),
             pltpu.VMEM((elements, width, node), BF16),
             pltpu.VMEM((2 * width + 32, entries), BF16),
             pltpu.VMEM((reach, width + 8, CAP), F32),
@@ -389,21 +409,27 @@
         compiler_params=pltpu.CompilerParams(collective_id=0, has_side_effects=True),
         name="step",
     )(
-        neighbors,
+        neighbors.T,
         basis_panel,
         jacobian,
         sample_rows.reshape(1, entries),
         residual_parts.reshape(1, entries),
     )
-    full_step = pl.pallas_call(
+    reduced_step, jacobian_basis, sampled_residual = pl.pallas_call(
         solve_kernel,
-        out_shape=shape((1, size), F32),
-        in_specs=[VMEM],
-        out_specs=VMEM,
+        out_shape=(
+            shape((1, width), F32), shape((width, ROWS_DEV), F32), shape((1, ROWS_DEV), F32)
+        ),
+        in_specs=[SMEM, VMEM, VMEM, VMEM],
+        out_specs=(VMEM, VMEM, VMEM),
         name="solve",
-    )(whole.reshape(size, size))
-    reduced_step = lax.dynamic_slice_in_dim(full_step[0], col_index * width, width)
-    return (jacobian_basis, sampled_residual[0], reduced_step)
+    )(
+        col_index.astype(jnp.int32).reshape(1),
+        whole.reshape(size, size),
+        jacobian_basis,
+        sampled_residual,
+    )
+    return (jacobian_basis, sampled_residual[0], reduced_step[0])
 
 
 def solution(mesh):

time: 72.9 us -> 66 us (0.905)
  local copies, waits for them, and re-layouts: 5.55 us -> 0 us
  Pallas kernels: 66.5 us -> 65.1 us
    unnamed x3 -> x0, local copies, waits for them, and re-layouts: 4.32 us -> none
    dynamic_slice x1 -> x0, local copies, waits for them, and re-layouts: 1.24 us -> none  [body(): lax.dynamic_slice_in_dim(full_step[0], col_index * width, width)]
where the time goes in v3:
time: 66 us; the launch traced here: 65.8 us
  Pallas kernels  65.1 us (99%)
    pallas_call x1, Pallas kernels, body(): pl.pallas_call(functools.partial(step_kernel, dom_count, col_count, reach...  49.8 us
    pallas_call x1, Pallas kernels, body(): pl.pallas_call(solve_kernel, out_shape=(shape((1, width), F32), shape((wi...  15.3 us

profile of v3, /device:TPU:0, one launch (start us, length us, event | category | flops | bytes accessed | tf_op | source)
XLA Modules:
  0.0 65.8 jit_solution(16994235007004825490)
XLA Ops:
  0.6 49.8 %step.1 = (f32[64,1024]{1,0:T(8,128)}, f32[1,1024]{1,0:T(1,128)}, f32[32,8,256]{2,1,0:T(8,128)}) custom-call(s32[2,64]{1,0:T(2,128)} %bitcast.10, bf16[64,20480]{1,0:T(8,128)(2,1)} %panel_hbm.1, bf16[2,320,2048]{2,1,0:T(8,128)(2,1)} %blocks_hbm.1, s32[1,2048]{1,0:T(1,128)} %bitcast.8, f32[1,2048]{1,0:T(1,128)} %bitcast.9), custom_call_target="tpu_custom_call" | custom-call | tf_op jit(solution)/shard_map/step/pallas_call | solution.py:380
  50.5 15.3 %solve.1 = (f32[1,64]{1,0:T(1,128)}, f32[64,1024]{1,0:T(8,128)}, f32[1,1024]{1,0:T(1,128)}) custom-call(s32[1]{0:T(128)} %bitcast.col_ref, f32[256,256]{1,0:T(8,128)} %bitcast.7, f32[64,1024]{1,0:T(8,128)} %get-tuple-element.10.basis_ref, f32[1,1024]{1,0:T(1,128)} %get-tuple-element.11.residual_ref), custom_call_target="tpu_custom_call" | custom-call | tf_op jit(solution)/shard_map/solve/pallas_call | solution.py:418

commit v4 on v3

--- a/solution.py
+++ b/solution.py
@@ -69,8 +69,8 @@
 def step_kernel(
     dom_count, col_count, reach, links_ref, panel_hbm, blocks_hbm, rows_ref, parts_ref,
     basis_ref, residual_ref, gram_ref,
-    panel_ref, blocks_ref, load_sems, panels, terms, send, arrived, local, terms_in, landing, pieces, others, parts, sums, total,
-    whole, dom_sems, col_sems, sum_sems, all_sems,
+    panel_ref, blocks_ref, load_sems, panels, terms, send, arrived, local, terms_in, landing, pieces, others, parts, paired, team_parts,
+    sums, total, whole, dom_sems, col_sems, pair_sems, sum_sems, all_sems, relay_sems,
 ):
     dom, col = lax.axis_index("dom"), lax.axis_index("col")
     devices = dom_count * col_count
@@ -97,6 +97,13 @@
         index = fold(me + offset, devices)
         return index, (index // col_count, index % col_count)
 
+    side, mate = dom % 2, (dom // 2 * 2 + 1 - dom % 2, col)
+    team, spot = devices // 2, dom // 2 * col_count + col
+
+    def mate_at(offset):
+        index = fold(spot + offset, team)
+        return index, (index // col_count * 2 + side, index % col_count)
+
     def dom_copy(o):
         return remote(send.at[o - 1], arrived.at[o - 1], dom_sems, o - 1, (fold(dom + o, dom_count), col))
 
@@ -104,13 +111,20 @@
         there = fold(col + o, col_count)
         return remote(pieces.at[there], others.at[col], col_sems, o - 1, (dom, there))
 
+    def pair_copy():
+        return remote(parts.at[1 - side], paired, pair_sems, 0, mate)
+
     def sum_copy(o):
-        index, device = device_at(o)
-        return remote(parts.at[index], sums.at[o - 1], sum_sems, o - 1, device)
+        index, device = mate_at(o)
+        return remote(team_parts.at[index], sums.at[o - 1], sum_sems, o - 1, device)
 
     def all_copy(o):
-        _, device = device_at(o)
-        return remote(total, whole.at[me], all_sems, o - 1, device)
+        _, device = mate_at(o)
+        return remote(total, whole.at[side, spot], all_sems, o - 1, device)
+
+    def relay_copy(o):
+        place = whole.at[side, fold(spot - o + team, team)]
+        return remote(place, place, relay_sems, o, mate)
 
     panel_load = pltpu.make_async_copy(panel_hbm, panel_ref, load_sems.at[0])
     blocks_load = pltpu.make_async_copy(blocks_hbm, blocks_ref, load_sems.at[1])
@@ -239,35 +253,47 @@
     gram = jnp.where((row == size - 1) & (column < size - 1), gradient, gram)
     turned = pltpu.roll(jnp.broadcast_to(gradient, (8, size)), 1, axis=1)[:1]
     gram = jnp.where((row == size - 2) & (column == 0), turned, gram)
-    count, height, span = parts.shape
-    if span == size:
+    _, count, height, span = parts.shape
+    for half in range(2):
         for index in range(count):
-            parts[index] = gram[index * height : (index + 1) * height]
-    else:
-        for index in range(count):
-            start = index * span % size
-            parts[index] = gram[index * span // size][None, start : start + span]
-
-    @pl.loop(1, devices)
+            if span == size:
+                start = (half * count + index) * height
+                parts[half, index] = gram[start : start + height]
+            else:
+                start = (half * count + index) * span
+                lane = start % size
+                parts[half, index] = gram[start // size][None, lane : lane + span]
+    pair_copy().start()
+    pair_copy().wait_recv()
+    team_parts[...] = parts[side] + paired[...]
+
+    @pl.loop(1, team)
     def _(o):
         sum_copy(o).start()
 
-    @pl.loop(1, devices)
+    @pl.loop(1, team)
     def _(o):
         sum_copy(o).wait_recv()
 
-    mine = jnp.sum(sums[...], axis=0) + parts[me]
+    mine = jnp.sum(sums[...], axis=0) + team_parts[spot]
     total[...] = mine
 
-    @pl.loop(1, devices)
+    @pl.loop(1, team)
     def _(o):
         all_copy(o).start()
 
-    whole[me] = mine
-
-    @pl.loop(1, devices)
+    whole[side, spot] = mine
+    relay_copy(0).start()
+
+    @pl.loop(1, team)
     def _(o):
         all_copy(o).wait_recv()
+        relay_copy(o).start()
+
+    @pl.loop(0, team)
+    def _(o):
+        back = whole.at[1 - side, fold(spot - o + team, team)]
+        remote(back, back, relay_sems, o, mate).wait_recv()
 
     gram_ref[...] = whole[...]
     for o in range(1, reach + 1):
@@ -275,10 +301,16 @@
     for o in range(1, col_count):
         col_copy(o).wait_send()
 
-    @pl.loop(1, devices)
+    pair_copy().wait_send()
+
+    @pl.loop(1, team)
     def _(o):
         sum_copy(o).wait_send()
         all_copy(o).wait_send()
+
+    @pl.loop(0, team)
+    def _(o):
+        relay_copy(o).wait_send()
 
 
 def inverse(matrix):
@@ -345,10 +377,7 @@
 
     top, bottom = gradient[:, :half], gradient[:, half:]
     x_top, x_bottom = apply(top, bottom)
-    off_top = top - dot_nn(x_top, first, HIGHEST) - dot_nt(x_bottom, cross, HIGHEST)
-    off_bottom = bottom - dot_nn(x_top, cross, HIGHEST) - dot_nn(x_bottom, second, HIGHEST)
-    more_top, more_bottom = apply(off_top, off_bottom)
-    full = -jnp.concatenate([x_top + more_top, x_bottom + more_bottom], axis=1)[:1]
+    full = -jnp.concatenate([x_top, x_bottom], axis=1)[:1]
     width = out_ref.shape[1]
     out = jnp.zeros((1, width), F32)
     for index in range(size // width):
@@ -373,10 +402,11 @@
     reach = min(dom_count - 1, REACH_MOST)
     part = ROWS_DEV // col_count
     devices = dom_count * col_count
+    team = devices // 2
     if size % devices == 0:
-        chunk = (devices, size // devices, size)
+        chunk = (2, team, size // devices, size)
     else:
-        chunk = (devices, 1, size * size // devices)
+        chunk = (2, team, 1, size * size // devices)
     jacobian_basis, sampled_residual, whole = pl.pallas_call(
         functools.partial(step_kernel, dom_count, col_count, reach),
         out_shape=(
@@ -398,13 +428,17 @@
             pltpu.VMEM((col_count, width, part), F32),
             pltpu.VMEM((col_count, width, part), F32),
             pltpu.VMEM(chunk, F32),
-            pltpu.VMEM((devices - 1,) + chunk[1:], F32),
             pltpu.VMEM(chunk[1:], F32),
+            pltpu.VMEM(chunk[1:], F32),
+            pltpu.VMEM((team - 1,) + chunk[2:], F32),
+            pltpu.VMEM(chunk[2:], F32),
             pltpu.VMEM(chunk, F32),
             pltpu.SemaphoreType.DMA((2, reach)),
             pltpu.SemaphoreType.DMA((2, col_count - 1)),
-            pltpu.SemaphoreType.DMA((2, devices - 1)),
-            pltpu.SemaphoreType.DMA((2, devices - 1)),
+            pltpu.SemaphoreType.DMA((2, 1)),
+            pltpu.SemaphoreType.DMA((2, team - 1)),
+            pltpu.SemaphoreType.DMA((2, team - 1)),
+            pltpu.SemaphoreType.DMA((2, team)),
         ],
         compiler_params=pltpu.CompilerParams(collective_id=0, has_side_effects=True),
         name="step",

time: 66 us -> 61 us (0.924)
  Pallas kernels: 65.1 us -> 60.1 us
    pallas_call x1, Pallas kernels: 49.8 us -> 45.9 us  [body(): pl.pallas_call(functools.partial(step_kernel, dom_count, col_count, reach...]
    pallas_call x1, Pallas kernels: 15.3 us -> 14.1 us  [body(): pl.pallas_call(solve_kernel, out_shape=(shape((1, width), F32), shape((wi...]
where the time goes in v4:
time: 61 us; the launch traced here: 60.7 us
  Pallas kernels  60.1 us (99%)
  between operations  0.64 us (1%)
    pallas_call x1, Pallas kernels, body(): pl.pallas_call(functools.partial(step_kernel, dom_count, col_count, reach...  45.9 us
    pallas_call x1, Pallas kernels, body(): pl.pallas_call(solve_kernel, out_shape=(shape((1, width), F32), shape((wi...  14.1 us

profile of v4, /device:TPU:0, one launch (start us, length us, event | category | flops | bytes accessed | tf_op | source)
XLA Modules:
  0.0 60.7 jit_solution(3735773932658688988)
XLA Ops:
  0.6 45.9 %step.1 = (f32[64,1024]{1,0:T(8,128)}, f32[1,1024]{1,0:T(1,128)}, f32[2,16,8,256]{3,2,1,0:T(8,128)}) custom-call(s32[2,64]{1,0:T(2,128)} %bitcast.10, bf16[64,20480]{1,0:T(8,128)(2,1)} %panel_hbm.1, bf16[2,320,2048]{2,1,0:T(8,128)(2,1)} %blocks_hbm.1, s32[1,2048]{1,0:T(1,128)} %bitcast.8, f32[1,2048]{1,0:T(1,128)} %bitcast.9), custom_call_target="tpu_custom_call" | custom-call | tf_op jit(solution)/shard_map/step/pallas_call | solution.py:410
  46.6 14.1 %solve.1 = (f32[1,64]{1,0:T(1,128)}, f32[64,1024]{1,0:T(8,128)}, f32[1,1024]{1,0:T(1,128)}) custom-call(s32[1]{0:T(128)} %bitcast.col_ref, f32[256,256]{1,0:T(8,128)} %bitcast.7, f32[64,1024]{1,0:T(8,128)} %get-tuple-element.10.basis_ref, f32[1,1024]{1,0:T(1,128)} %get-tuple-element.11.residual_ref), custom_call_target="tpu_custom_call" | custom-call | tf_op jit(solution)/shard_map/solve/pallas_call | solution.py:452

commit v5 on v4

--- a/solution.py
+++ b/solution.py
@@ -163,7 +163,7 @@
 
     panel_load.wait()
 
-    @pl.loop(0, elements // 2)
+    @pl.loop(0, elements // 2, unroll=4)
     def _(pair):
         window = panel_ref[:, pl.ds(pl.multiple_of(pair * 2 * node, LANES), 2 * node)]
         panels[2 * pair] = window[:, :node]
@@ -173,7 +173,7 @@
 
     blocks_load.wait()
 
-    @pl.loop(0, elements // group)
+    @pl.loop(0, elements // group, unroll=4)
     def _(block):
         columns = pl.ds(pl.multiple_of(block * LANES, LANES), LANES)
         found = jnp.zeros((group * width, LANES), F32)
@@ -341,7 +341,7 @@
         return tuple(pltpu.roll(x, size - 8, axis=1) for x in done + [work])
 
     groups = tuple(matrix[k : k + 8] for k in range(0, size, 8))
-    return jnp.concatenate(lax.fori_loop(0, size // 8, step, groups, unroll=2), axis=0)
+    return jnp.concatenate(lax.fori_loop(0, size // 8, step, groups, unroll=4), axis=0)
 
 
 def solve_kernel(

time: 61 us -> 56.8 us (0.931)
  Pallas kernels: 60.1 us -> 55.9 us
    pallas_call x1, Pallas kernels: 45.9 us -> 42.2 us  [body(): pl.pallas_call(functools.partial(step_kernel, dom_count, col_count, reach...]
where the time goes in v5:
time: 56.8 us; the launch traced here: 56.5 us
  Pallas kernels  55.9 us (98%)
  between operations  0.64 us (1%)
    pallas_call x1, Pallas kernels, body(): pl.pallas_call(functools.partial(step_kernel, dom_count, col_count, reach...  42.2 us
    pallas_call x1, Pallas kernels, body(): pl.pallas_call(solve_kernel, out_shape=(shape((1, width), F32), shape((wi...  13.7 us

profile of v5, /device:TPU:0, one launch (start us, length us, event | category | flops | bytes accessed | tf_op | source)
XLA Modules:
  0.0 56.5 jit_solution(8432187601881481000)
XLA Ops:
  0.6 42.2 %step.1 = (f32[64,1024]{1,0:T(8,128)}, f32[1,1024]{1,0:T(1,128)}, f32[2,16,8,256]{3,2,1,0:T(8,128)}) custom-call(s32[2,64]{1,0:T(2,128)} %bitcast.10, bf16[64,20480]{1,0:T(8,128)(2,1)} %panel_hbm.1, bf16[2,320,2048]{2,1,0:T(8,128)(2,1)} %blocks_hbm.1, s32[1,2048]{1,0:T(1,128)} %bitcast.8, f32[1,2048]{1,0:T(1,128)} %bitcast.9), custom_call_target="tpu_custom_call" | custom-call | tf_op jit(solution)/shard_map/step/pallas_call | solution.py:410
  42.8 13.7 %solve.1 = (f32[1,64]{1,0:T(1,128)}, f32[64,1024]{1,0:T(8,128)}, f32[1,1024]{1,0:T(1,128)}) custom-call(s32[1]{0:T(128)} %bitcast.col_ref, f32[256,256]{1,0:T(8,128)} %bitcast.7, f32[64,1024]{1,0:T(8,128)} %get-tuple-element.10.basis_ref, f32[1,1024]{1,0:T(1,128)} %get-tuple-element.11.residual_ref), custom_call_target="tpu_custom_call" | custom-call | tf_op jit(solution)/shard_map/solve/pallas_call | solution.py:452
